TPU v7x, 32 devices: a whole 2x2x4 slice. The times are simulated.
32 devices in a mesh: member: 4 (over y, x), grid: 8 (over z, core).
Axes of the slice: x: 2, y: 2, z: 4, core: 2. Of those that a mesh axis runs over, the one named last changes fastest.
Arguments:
- latent: bfloat16 [4, 16384, 1024], P('member', 'grid'), may hold values from -6 to 6
- w_in: bfloat16 [1024, 1024], P(('member', 'grid')), may hold values from -0.1875 to 0.1875
- b_in: float32 [1024], replicated, may hold values from -3 to 3
- w_out: bfloat16 [100, 1024], replicated, may hold values from -0.1875 to 0.1875
- b_out: float32 [100], replicated, may hold values from -3 to 3
- targets: float32 [100, 16384], P(None, 'grid'), may hold values from -6 to 6
- var_weight: float32 [100], replicated, may hold values from 0.5 to 5
- plan: int32 [3, 4], replicated, may hold values from 0 to 3, as said below
Outputs:
- loss: float32 [], replicated
- grad_latent: bfloat16 [4, 16384, 1024], P('member', 'grid')
- grad_w_in: float32 [1024, 1024], P(('member', 'grid'))
- grad_b_in: float32 [1024], replicated
- grad_w_out: float32 [100, 1024], replicated
- grad_b_out: float32 [100], replicated
Inputs may be any that keep to these rules, and one draw needn't show every extreme that they name: `plan`: each row is a perfect pairing of the 4 members: no member is its own partner, the partner of a member's partner is the member, and no pair occurs in two rows.
All inputs are finite; a program needn't handle non-finite values.
Results may differ from a plain program's by a relative error of at most 0.0095.
Values may be sent and summed in bfloat16 or wider, within the bound.
A program may use at most 128 MiB of HBM per device.

v0:
```python
import jax
import jax.numpy as jnp
from jax import lax
from jax.sharding import PartitionSpec as P

DELTA = 0.25


def make_fold(mine, partner_rows):

    def fold(carry, piece, start):
        count = piece.shape[0]
        labels = jnp.arange(count, dtype=jnp.int32)
        weights = jnp.sum((partner_rows[:, None] == labels[None, :]).astype(jnp.float32), axis=0)
        diff = mine[None] - piece
        root = jnp.sqrt(diff * diff + DELTA * DELTA)
        slope_sum = jnp.einsum("k,kvp->vp", weights, diff / root)
        spread_sum = jnp.einsum("k,kvp->vp", weights, root - DELTA)
        return (slope_sum, spread_sum)

    return fold


def shards(latent, w_in, b_in, w_out, b_out, targets, var_weight, plan):
    hidden_in = latent[0]
    points = hidden_in.shape[0]
    rounds = plan.shape[0]
    w_full = lax.all_gather(w_in, ("member", "grid"), axis=0, tiled=True)
    member = lax.axis_index("member")
    grid_index = lax.axis_index("grid")
    members = lax.axis_size("member")
    grid_count = lax.axis_size("grid")
    total = points * grid_count
    place = (grid_index * points + jnp.arange(points, dtype=jnp.int32)).astype(jnp.float32)
    area = jnp.cos(1.4 * (place + 0.5) / total)
    scale_map = area[None, :] * var_weight[:, None]
    partner_rows = lax.dynamic_index_in_dim(plan, member, 1, keepdims=False)
    pre = jnp.dot(hidden_in, w_full, preferred_element_type=jnp.float32) + b_in[None, :]
    act = jax.nn.gelu(pre).astype(jnp.bfloat16)
    field = jnp.dot(w_out, act.T, preferred_element_type=jnp.float32) + b_out[:, None]
    pre, act, field = (pre, act, field)
    fold_all = make_fold(field, partner_rows)
    slope_sum, spread_sum = fold_all(
        (
            jnp.zeros((w_out.shape[0], points), jnp.float32),
            jnp.zeros((w_out.shape[0], points), jnp.float32),
        ),
        lax.all_gather(field[None], "member", axis=0, tiled=True),
        jnp.int32(0),
    )
    miss = field - targets
    miss_root = jnp.sqrt(miss * miss + DELTA * DELTA)
    cot = scale_map * (miss / miss_root - slope_sum / rounds)
    terms = scale_map * (miss_root - DELTA - spread_sum / (2.0 * rounds))
    cot_b = cot.astype(jnp.bfloat16)
    dact = jnp.dot(cot_b.T, w_out, preferred_element_type=jnp.float32)
    _, pull = jax.vjp(jax.nn.gelu, pre)
    dpre = pull(dact)[0]
    dpre_b = dpre.astype(jnp.bfloat16)
    grad_hidden = jnp.dot(dpre_b, w_full.T, preferred_element_type=jnp.float32).astype(jnp.bfloat16)
    kappa = 4.0 / jnp.sqrt(jnp.float32(members * total))
    out_term = jnp.dot(cot_b, act, preferred_element_type=jnp.float32)
    sum_w2, sum_b2, sum_b1, sum_loss = lax.psum(
        (out_term, jnp.sum(cot, axis=1), jnp.sum(dpre, axis=0), jnp.sum(terms)), ("member", "grid")
    )
    row_count = w_in.shape[0]
    full_term = jnp.dot(hidden_in.T, dpre_b, preferred_element_type=jnp.float32)
    summed = lax.psum(full_term, ("member", "grid"))
    offset = (member * grid_count + grid_index) * row_count
    own_rows = lax.dynamic_slice_in_dim(summed, offset, row_count, 0)
    loss = sum_loss / (members * total * w_out.shape[0])
    return (
        loss,
        grad_hidden[None],
        own_rows * kappa,
        sum_b1 * kappa,
        sum_w2 * kappa,
        sum_b2 * kappa,
    )


def solution(mesh):
    placed = (
        P("member", "grid", None),
        P(("member", "grid"), None),
        P(),
        P(),
        P(),
        P(None, "grid"),
        P(),
        P(),
    )
    return jax.shard_map(
        shards,
        mesh=mesh,
        in_specs=placed,
        out_specs=(P(), P("member", "grid", None), P(("member", "grid"), None), P(), P(), P()),
        check_vma=False,
    )
```

profile of v0, /device:TPU:0, one launch (start us, length us, event | category | flops | bytes accessed | tf_op | source)
XLA Modules:
  0.0 314.8 jit_solution(176312685876041185)
XLA Ops:
  7.2 0.7 all-gather.5.cloned.1.call-update
  8.0 62.1 %all-gather.5.cloned.1.call-done = bf16[1024,1024]{1,0:T(8,128)(2,1)} async-done(((bf16[32,1024]{1,0:T(8,128)(2,1)}), bf16[1024,1024]{1,0:T(8,128)(2,1)}) %all-gather.5.cloned.1.call-update) | async-done | bytes 2097168 | tf_op jit(solution)/shard_map/all_gather | solution.py:28
  70.1 12.6 %multiply_convert_fusion = (bf16[2048,1024]{1,0:T(8,128)(2,1)S(1)}, f32[2048,1024]{1,0:T(8,128)}) fusion(f32[1024]{0:T(1024)} %param.10, bf16[1024,1024]{1,0:T(8,128)(2,1)} %all-gather.5.cloned.1.call-done, bf16[1,2048,1024]{2,1,0:T(8,128)(2,1)} %param.8), kind=kOutput, calls=%fused_computation.8 | convolution fusion | flops 4315938816 | bytes 18878464 | tf_op jit(solution)/shard_map/dot_general | solution.py:38
  82.7 2.0 copy-done.1
  84.8 2.4 convolution_add_fusion
  87.1 0.2 all-reduce.4.cloned.1.call-start
  87.4 0.2 dynamic-slice_reduce_fusion
  87.7 44.5 %all-gather.7.cloned.1.call-done = f32[4,100,2048]{2,1,0:T(8,128)} async-done(((f32[1,100,2048]{2,1,0:T(8,128)}), f32[4,100,2048]{2,1,0:T(8,128)}) %all-gather.7.cloned.1.call-update) | async-done | bytes 3276816 | tf_op jit(solution)/shard_map/all_gather | solution.py:48
  132.2 4.1 %fusion.10 = (bf16[4,100,2048]{2,1,0:T(8,128)(2,1)S(1)}, bf16[4,100,2048]{2,1,0:T(8,128)(2,1)S(1)}) fusion(f32[4,100,2048]{2,1,0:T(8,128)} %all-gather.7.cloned.1.call-done, f32[100,2048]{1,0:T(8,128)} %bitcast.49), kind=kLoop, calls=%fused_computation.15 | loop fusion | flops 5734400 | bytes 7372800 | tf_op jit(solution)/shard_map/div | solution.py:17
  136.3 1.3 fusion.12
  137.7 1.3 fusion.14
  139.1 1.9 fusion.29
  140.9 1.6 fusion.24
  142.5 7.0 %fusion.30 = (f32[1024]{0:T(1024)S(1)}, bf16[2048,1024]{1,0:T(8,128)(2,1)S(1)}) fusion(f32[2048,1024]{1,0:T(8,128)S(1)} %bitcast.51, f32[1024]{0:T(1024)S(1)} %copy-done.10, bf16[100,1024]{1,0:T(8,128)(2,1)S(1)} %copy-done, bf16[100,2048]{1,0:T(8,128)(2,1)S(1)} %get-tuple-element.30), kind=kOutput, calls=%fused_computation.47 | convolution fusion | flops 465566720 | bytes 13205504 | tf_op jit(solution)/shard_map/dot_general | solution.py:56
  149.5 2.0 copy-done.11
  151.5 6.2 %fusion.16 = f32[1024,1024]{0,1:T(8,128)} fusion(bf16[1,2048,1024]{2,1,0:T(8,128)(2,1)S(1)} %copy-done.8, bf16[2048,1024]{1,0:T(8,128)(2,1)S(1)} %get-tuple-element.37), kind=kOutput, calls=%fused_computation.22 | convolution fusion | flops 4294967296 | bytes 12582912 | tf_op jit(solution)/shard_map/dot_general | solution.py:67
  157.7 40.3 %all-reduce = (f32[]{:T(128)}, f32[1024]{0:T(1024)S(1)}, f32[100]{0:T(128)S(1)}) all-reduce(f32[]{:T(128)} %get-tuple-element.33, f32[1024]{0:T(1024)S(1)} %get-tuple-element.36, f32[100]{0:T(128)S(1)} %get-tuple-element.29), channel_id=1, replica_groups=mesh['member'=4,'grid'=8] {'member','grid'}, use_global_device_ids=true, to_apply=%region_2.3 | all-reduce | flops 1125 | bytes 9000 | tf_op jit(solution)/shard_map/psum | solution.py:63
  198.7 0.5 broadcast_multiply_fusion.2
  199.2 0.6 broadcast_multiply_fusion.1
  199.8 8.3 %convert_bitcast_fusion = bf16[1,2048,1024]{2,1,0:T(8,128)(2,1)} fusion(bf16[1024,1024]{1,0:T(8,128)(2,1)S(1)} %copy-done.9, bf16[2048,1024]{1,0:T(8,128)(2,1)} %copy-done.11), kind=kOutput, calls=%fused_computation.13 | convolution fusion | flops 4297064448 | bytes 10485760 | tf_op jit(solution)/shard_map/dot_general | solution.py:60
  208.1 95.1 %all-reduce.4.cloned.1.call-done = (f32[1024,1024]{0,1:T(8,128)}, f32[100,1024]{1,0:T(8,128)}) async-done(((f32[1024,1024]{0,1:T(8,128)}, f32[100,1024]{1,0:T(8,128)}), (f32[1024,1024]{0,1:T(8,128)}, f32[100,1024]{1,0:T(8,128)})) %all-reduce.4.cloned.1.call-update) | async-done | bytes 4603920 | tf_op jit(solution)/shard_map/psum | solution.py:68
  303.2 1.2 dynamic-slice_multiply_fusion
  304.5 0.8 copy.16
  305.3 1.8 broadcast_multiply_fusion
  (33 shorter events, 0.3 us)
Async XLA Ops:
  7.2 77.6 %copy-start = (bf16[100,1024]{1,0:T(8,128)(2,1)S(1)}, bf16[100,1024]{1,0:T(8,128)(2,1)}, u32[]{:S(2)}) copy-start(bf16[100,1024]{1,0:T(8,128)(2,1)} %param.11) | copy-start | bytes 614404
  7.2 62.9 %all-gather.5.cloned.1.call-start = ((), (), s32[]{:S(2)}) async-start(), calls=%async_computation | async-start | bytes 2162688 | tf_op jit(solution)/shard_map/all_gather | solution.py:28
  7.9 76.8 %copy-start.5 = (f32[100]{0:T(128)S(1)}, f32[100]{0:T(128)}, u32[]{:S(2)}) copy-start(f32[100]{0:T(128)} %param.12) | copy-start | bytes 1204
  7.9 124.3 %all-gather.7.cloned.1.call-start = ((), (), s32[]{:S(2)}) async-start(), calls=%async_computation.1 | async-start | bytes 4259840 | tf_op jit(solution)/shard_map/all_gather | solution.py:48
  82.7 2.0 copy-start.1
  82.7 4.6 %copy-start.6 = (s32[3,4]{1,0:T(4,128)S(1)}, s32[3,4]{1,0:T(4,128)}, u32[]{:S(2)}) copy-start(s32[3,4]{1,0:T(4,128)} %param.15) | copy-start | bytes 148
  87.1 216.1 %all-reduce.4.cloned.1.call-start = ((), (), s32[]{:S(2)}) async-start(), calls=%async_computation.2 | async-start | bytes 9240576 | tf_op jit(solution)/shard_map/psum | solution.py:68
  132.2 10.3 %slice-start = ((s8[8388608]{0:T(1024)(128)(4,1)}), s8[4194304]{0:T(1024)(128)(4,1)S(1)}, s32[]{:S(2)}) async-start(s8[8388608]{0:T(1024)(128)(4,1)} %bitcast.50), calls=%async_computation.3 | async-start | bytes 8388608
  136.3 2.7 copy-start.3
  136.3 2.7 copy-start.4
  136.3 2.7 copy-start.7
  137.7 3.3 %copy-start.2 = (bf16[2048,1024]{1,0:T(8,128)(2,1)S(1)}, bf16[2048,1024]{1,0:T(8,128)(2,1)}, u32[]{:S(2)}) copy-start(bf16[2048,1024]{1,0:T(8,128)(2,1)} %copy-done.1) | copy-start | bytes 12582916
  137.7 4.8 %slice-start.1 = ((s8[8388608]{0:T(1024)(128)(4,1)}), s8[4194304]{0:T(1024)(128)(4,1)S(1)}, s32[]{:S(2)}) async-start(s8[8388608]{0:T(1024)(128)(4,1)} %bitcast.50), calls=%async_computation.4 | async-start | bytes 8388608
  139.0 3.4 %copy-start.10 = (f32[1024]{0:T(1024)S(1)}, f32[1024]{0:T(1024)}, u32[]{:S(2)}) copy-start(f32[1024]{0:T(1024)} %param.10) | copy-start | bytes 12292
  142.5 9.0 %copy-start.8 = (bf16[1,2048,1024]{2,1,0:T(8,128)(2,1)S(1)}, bf16[1,2048,1024]{2,1,0:T(8,128)(2,1)}, u32[]{:S(2)}) copy-start(bf16[1,2048,1024]{2,1,0:T(8,128)(2,1)} %param.8) | copy-start | bytes 12582916
  149.5 2.0 copy-start.11
  157.7 42.1 %copy-start.9 = (bf16[1024,1024]{1,0:T(8,128)(2,1)S(1)}, bf16[1024,1024]{1,0:T(8,128)(2,1)}, u32[]{:S(2)}) copy-start(bf16[1024,1024]{1,0:T(8,128)(2,1)} %all-gather.5.cloned.1.call-done) | copy-start | bytes 6291460
Sparse Core Ops, SparseCore 0:
  11.0 59.0 all-gather.4
  87.3 44.8 all-gather.6
  157.8 145.3 all-reduce.3
where the time goes:
time: 315 us
  waiting for transfers between devices  202 us (64%)
  matrix products  40.7 us (13%)
  blocking collectives  40.3 us (13%)
  between operations  15.7 us (5%)
  other arithmetic  10.2 us (3%)
  local copies, waits for them, and re-layouts  5.12 us (2%)
    psum x1, waiting for transfers between devices, shards(): summed = lax.psum(full_term, ('member', 'grid'))  95.1 us
    all_gather x1, waiting for transfers between devices, shards(): w_full = lax.all_gather(w_in, ('member', 'grid'), axis=0, tiled=True)  62.1 us
    all_gather x1, waiting for transfers between devices, shards(): lax.all_gather(field[None], 'member', axis=0, tiled=True)  44.5 us
    psum x1, blocking collectives, shards(): lax.psum((out_term, jnp.sum(cot, axis=1), jnp.sum(dpre, axis=0), jnp.sum(...  40.3 us
    dot_general x1, matrix products, shards(): jnp.dot(hidden_in, w_full, preferred_element_type=jnp.float32)  12.6 us
    dot_general x1, matrix products, shards(): jnp.dot(dpre_b, w_full.T, preferred_element_type=jnp.float32)  8.35 us
    dot_general x1, matrix products, shards(): dact = jnp.dot(cot_b.T, w_out, preferred_element_type=jnp.float32)  6.99 us
  transfers between devices with their start and end apart: 3, of which 3 were waited for; matrix products, arithmetic and copies ran while one was open for 3% of the time, Pallas kernels for 0%

commit v1 on v0

--- a/solution.py
+++ b/solution.py
@@ -1,6 +1,11 @@
+import functools
+import math
+
 import jax
 import jax.numpy as jnp
 from jax import lax
+from jax.experimental import pallas as pl
+from jax.experimental.pallas import tpu as pltpu
 from jax.sharding import PartitionSpec as P
 
 DELTA = 0.25
@@ -79,6 +84,399 @@
     )
 
 
+TILE = 256
+LANES = 128
+BF = jnp.bfloat16
+F32 = jnp.float32
+
+
+def dot(a, b, dims):
+    return lax.dot_general(a, b, (dims, ((), ())), preferred_element_type=F32)
+
+
+NN = ((1,), (0,))
+NT = ((1,), (1,))
+TN = ((0,), (0,))
+
+
+def head_kernel(
+    members, planes, lat_hbm, w_in, b_in, w_out, b_out, tgt_hbm, vw,
+    gh_hbm, g_w1, g_b1, g_w2, g_b2, g_loss,
+    lat, lat_t, w_buf, gp, act, dpre, gh, fsend, frecv, csend, crecv, tgt, rowbuf, lane_sums,
+    ot, op_send, op_recv, om_keep, om_send, om_recv, oz, w2, sm, sp_recv, smm, smz,
+    keep, p_send, p_recv, m_send, m_recv, z_keep, z_send, z_recv,
+    send_sem, recv_sem, local_sem, out_sem,
+):
+    m = lax.axis_index("member")
+    g = lax.axis_index("grid")
+    z, c = g // 2, lax.rem(g, 2)
+    other = 1 - c
+    points = lat.shape[1]
+    width = lat.shape[2]
+    sub = points // members
+    rows = w_in.shape[0]
+    vars_ = w_out.shape[0]
+    latent = w_out.shape[1]
+    total = points * planes * 2
+
+    def mem(k):
+        return lax.rem(m + k + members, members)
+
+    def zed(k):
+        return lax.rem(z + k + planes, planes)
+
+    partner = (m, z * 2 + other)
+
+    def member_dev(k):
+        return (mem(k), g)
+
+    def z_dev(k):
+        return (m, zed(k) * 2 + c)
+
+    started = []
+
+    def send(src, dst, dev):
+        n = len(started)
+        copy = pltpu.make_async_remote_copy(
+            src_ref=src, dst_ref=dst, send_sem=send_sem.at[n], recv_sem=recv_sem.at[n],
+            device_id=dev, device_id_type=pl.DeviceIdType.MESH,
+        )
+        copy.start()
+        started.append(copy)
+        return copy
+
+    loads = []
+    for ch in range(members):
+        copy = pltpu.make_async_copy(
+            lat_hbm.at[0, :, pl.ds(ch * width, width)], lat.at[ch], local_sem.at[ch]
+        )
+        copy.start()
+        loads.append(copy)
+    own = pltpu.make_async_copy(w_in, w_buf.at[m, z, c], local_sem.at[members])
+    own.start()
+    tgt_copy = pltpu.make_async_copy(
+        tgt_hbm.at[:, pl.ds(pl.multiple_of(m * sub, LANES), sub)], tgt, local_sem.at[members + 1]
+    )
+    tgt_copy.start()
+
+    barrier = pltpu.get_barrier_semaphore()
+    peers = [partner] + [z_dev(k) for k in range(1, planes)] + [member_dev(k) for k in range(1, members)]
+    for dev in peers:
+        pl.semaphore_signal(barrier, inc=1, device_id=dev, device_id_type=pl.DeviceIdType.MESH)
+    pl.semaphore_wait(barrier, len(peers))
+
+    z_copies = [send(w_in, w_buf.at[m, z, c], z_dev(k)) for k in range(1, planes)]
+
+    for copy in loads:
+        copy.wait()
+    own.wait()
+    for copy in z_copies:
+        copy.wait_recv()
+    half = w_buf.at[m, :, c]
+    mem_copies = [None] + [send(half, half, member_dev(k)) for k in range(1, members)]
+    part_copies = [send(half, half, partner)]
+
+    def transpose_chunk(ch):
+        def body(t, carry):
+            r0 = pl.multiple_of(t * TILE, TILE)
+            lat_t[ch, :, pl.ds(r0, TILE)] = lat[ch, pl.ds(r0, TILE), :].T
+            return carry
+        lax.fori_loop(0, points // TILE, body, 0)
+
+    for ch in range(members):
+        transpose_chunk(ch)
+    rowbuf[...] = jnp.zeros_like(rowbuf)
+    rowbuf[0:1, :vars_] = b_out[...]
+    rowbuf[1:2, :vars_] = vw[...]
+    b_col = jnp.broadcast_to(rowbuf[0:1, :], (LANES, LANES)).T[:vars_]
+    v_col = jnp.broadcast_to(rowbuf[1:2, :], (LANES, LANES)).T[:vars_]
+    lane_sums[...] = jnp.zeros_like(lane_sums)
+    ot[...] = jnp.zeros_like(ot)
+    sm[...] = jnp.zeros_like(sm)
+
+    for k in range(members):
+        ch = mem(-k)
+        if k > 0:
+            mem_copies[k].wait_recv()
+            got = w_buf.at[ch, :, c]
+            part_copies.append(send(got, got, partner))
+        part_copies[k].wait_recv()
+        if k == members - 1:
+            break
+
+        def body(t, carry, ch=ch, first=k == 0):
+            r0 = pl.multiple_of(t * TILE, TILE)
+            w = w_buf[ch].reshape(width, latent)
+            before = b_in[...] if first else gp[pl.ds(r0, TILE), :]
+            gp[pl.ds(r0, TILE), :] = before + dot(lat[ch, pl.ds(r0, TILE), :], w, NN)
+            return carry
+
+        lax.fori_loop(0, points // TILE, body, 0)
+
+    last = mem(1 - members)
+    c0 = math.sqrt(2.0 / math.pi)
+    f_copies = [None]
+    for k in range(1, members + 1):
+        base = mem(k) * sub
+
+        def body(t, carry, base=base):
+            r0 = pl.multiple_of(base + t * TILE, TILE)
+            x = dot(lat[last, pl.ds(r0, TILE), :], w_buf[last].reshape(width, latent), NN)
+            x = x + (b_in[...] if members == 1 else gp[pl.ds(r0, TILE), :])
+            sq = x * x
+            th = jnp.tanh(c0 * x * (1.0 + 0.044715 * sq))
+            cdf = 0.5 + 0.5 * th
+            act[pl.ds(r0, TILE), :] = (x * cdf).astype(BF)
+            gp[pl.ds(r0, TILE), :] = cdf + 0.5 * x * (1.0 - th * th) * (c0 + (3.0 * 0.044715 * c0) * sq)
+            return carry
+
+        lax.fori_loop(0, sub // TILE, body, 0)
+        field = dot(w_out[...], act[pl.ds(pl.multiple_of(base, TILE), sub), :], NT)
+        if k < members:
+            fsend[k - 1] = field
+            f_copies.append(send(fsend.at[k - 1], frecv.at[k], member_dev(k)))
+        else:
+            frecv[0] = field
+
+    tgt_copy.wait()
+    for k in range(1, members):
+        f_copies[k].wait_recv()
+    eps = DELTA * DELTA
+    b_sum = jnp.zeros((vars_, LANES), F32)
+    l_sum = jnp.zeros((vars_, LANES), F32)
+    for t in range(sub // LANES):
+        cols = slice(t * LANES, (t + 1) * LANES)
+        place = lax.broadcasted_iota(jnp.int32, (1, LANES), 1) + (g * points + m * sub + t * LANES)
+        area = jnp.cos(1.4 * (place.astype(F32) + 0.5) / total)
+        scale = v_col * area
+        f = [frecv[k, :, cols] for k in range(members)]
+        goal = tgt[:, cols] - b_col
+        pairs = [None] * members
+        spread = jnp.zeros((vars_, LANES), F32)
+        for a in range(members):
+            for b in range(a + 1, members):
+                d = f[a] - f[b]
+                q = d * d + eps
+                inv = lax.rsqrt(q)
+                s = d * inv
+                spread += q * inv - DELTA
+                pairs[a] = s if pairs[a] is None else pairs[a] + s
+                pairs[b] = -s if pairs[b] is None else pairs[b] - s
+        miss_sum = jnp.zeros((vars_, LANES), F32)
+        for a in range(members):
+            d = f[a] - goal
+            q = d * d + eps
+            inv = lax.rsqrt(q)
+            miss_sum += q * inv - DELTA
+            cot = scale * (d * inv - pairs[a] * (1.0 / (members - 1)))
+            b_sum += cot
+            if a == 0:
+                crecv[0, :, cols] = cot.astype(BF)
+            else:
+                csend[a - 1, :, cols] = cot.astype(BF)
+        l_sum += scale * (miss_sum - spread * (1.0 / (members - 1)))
+    c_copies = [None] + [send(csend.at[a - 1], crecv.at[a], member_dev(-a)) for a in range(1, members)]
+    lane_sums[:vars_, :] = b_sum
+    sm[1:2, :LANES] = jnp.sum(lane_sums[...].T, axis=0, keepdims=True)
+    sm[1:2, LANES:2 * LANES] = jnp.sum(l_sum, axis=0, keepdims=True)
+
+    col = jnp.zeros((1, latent), F32)
+    for a in range(members):
+        if a > 0:
+            c_copies[a].wait_recv()
+        base = mem(a) * sub
+
+        def body(t, carry, base=base, a=a):
+            r0 = pl.multiple_of(base + t * TILE, TILE)
+            cot_b = crecv[a, :, pl.ds(pl.multiple_of(t * TILE, TILE), TILE)]
+            d = dot(cot_b, w_out[...], TN) * gp[pl.ds(r0, TILE), :]
+            dpre[pl.ds(r0, TILE), :] = d.astype(BF)
+            ot[:vars_, :] += dot(cot_b, act[pl.ds(r0, TILE), :], NN)
+            return carry + jnp.sum(d, axis=0, keepdims=True)
+
+        col = lax.fori_loop(0, sub // TILE, body, col)
+    sm[0:1, :] = col
+
+    share = ot.shape[0] // (2 * members)
+    first_half = pl.multiple_of(other * (members * share), share)
+    op_send[...] = ot[pl.ds(first_half, members * share), :].astype(BF)
+    op_copy = send(op_send, op_recv, partner)
+    sp_copy = send(sm, sp_recv, partner)
+
+    def chunk(k):
+        t = mem(k)
+        part = dot(lat_t[t], dpre[...], NN).reshape(planes, 2, rows, latent)
+        gather_ref = keep
+        gather_ref[...] = part
+        p_send[k - 1] = keep[:, other].astype(BF)
+        m_keep_k = keep[:, c]
+        return m_keep_k, send(p_send.at[k - 1], p_recv.at[k - 1], partner)
+
+    def chip_sum(k, mine, copy):
+        copy.wait_recv()
+        return mine + p_recv[k - 1].astype(F32)
+
+    def to_member(k):
+        p_copies[k].wait_recv()
+        m_send[k - 1] = (z_keep[k - 1] + p_recv[k - 1].astype(F32)).astype(BF)
+        return send(m_send.at[k - 1], m_recv.at[k - 1], member_dev(k))
+
+    p_copies = {}
+    m_copies = {}
+
+    def do_chunk(k):
+        mine, copy = chunk(k)
+        z_keep[k - 1] = mine
+        p_copies[k] = copy
+
+    do_chunk(1)
+    op_copy.wait_recv()
+    mine = pl.multiple_of(c * (members * share), share)
+    om_keep[...] = (ot[pl.ds(mine, members * share), :] + op_recv[...].astype(F32)).reshape(members, share, latent)
+    om_send[...] = om_keep[...].astype(BF)
+    om_copies = [send(om_send.at[mem(k)], om_recv.at[k - 1], member_dev(k)) for k in range(1, members)]
+    sp_copy.wait_recv()
+    smm[m] = sm[...] + sp_recv[...]
+    sm_copies = [send(smm.at[m], smm.at[m], member_dev(k)) for k in range(1, members)]
+    do_chunk(2)
+    m_copies[1] = to_member(1)
+    acc = om_keep[m]
+    for k in range(1, members):
+        om_copies[k - 1].wait_recv()
+        acc += om_recv[k - 1].astype(F32)
+    oz[z] = acc.astype(BF)
+    oz_copies = [send(oz.at[z], oz.at[z], z_dev(k)) for k in range(1, planes)]
+    for copy in sm_copies:
+        copy.wait_recv()
+    acc = smm[0]
+    for k in range(1, members):
+        acc += smm[k]
+    smz[z] = acc
+    sz_copies = [send(smz.at[z], smz.at[z], z_dev(k)) for k in range(1, planes)]
+    for k in range(3, members):
+        do_chunk(k)
+        m_copies[k - 1] = to_member(k - 1)
+    for copy in oz_copies:
+        copy.wait_recv()
+    acc = oz[0].astype(F32)
+    for k in range(1, planes):
+        acc += oz[k].astype(F32)
+    w2[c, m] = acc
+    w2_copies = [send(w2.at[c, m], w2.at[c, m], member_dev(k)) for k in range(1, members)]
+    do_chunk(members)
+    m_copies[members - 1] = to_member(members - 1)
+    for copy in w2_copies:
+        copy.wait_recv()
+    half_copy = send(w2.at[c], w2.at[c], partner)
+
+    outs = []
+    for ch in range(members):
+        def body(t, carry, ch=ch):
+            r0 = pl.multiple_of(t * TILE, TILE)
+            w = w_buf[ch].reshape(width, latent)
+            gh[ch, pl.ds(r0, TILE), :] = dot(dpre[pl.ds(r0, TILE), :], w, NT).astype(BF)
+            return carry
+
+        lax.fori_loop(0, points // TILE, body, 0)
+        copy = pltpu.make_async_copy(gh.at[ch], gh_hbm.at[0, :, pl.ds(ch * width, width)], out_sem.at[ch])
+        copy.start()
+        outs.append(copy)
+
+    kappa = 4.0 / math.sqrt(members * total)
+    p_copies[members].wait_recv()
+    acc = z_keep[members - 1] + p_recv[members - 1].astype(F32)
+    for k in range(1, members):
+        m_copies[k].wait_recv()
+        acc += m_recv[k - 1].astype(F32)
+    z_keep[members - 1] = acc
+    z_send[...] = acc.astype(BF)
+    zz_copies = [send(z_send.at[zed(k)], z_recv.at[k - 1], z_dev(k)) for k in range(1, planes)]
+
+    for copy in sz_copies:
+        copy.wait_recv()
+    acc = smz[0]
+    for k in range(1, planes):
+        acc += smz[k]
+    acc = acc * kappa
+    g_b1[...] = acc[0:1, :]
+    g_b2[...] = acc[1:2, :vars_]
+    g_loss[...] = jnp.sum(acc[1:2, LANES:2 * LANES], axis=1, keepdims=True) * (1.0 / (kappa * members * total * vars_))
+    half_copy.wait_recv()
+    g_w2[...] = w2[...].reshape(2 * members * share, latent)[:vars_] * kappa
+
+    acc = z_keep[members - 1, z]
+    for k in range(1, planes):
+        zz_copies[k - 1].wait_recv()
+        acc += z_recv[k - 1].astype(F32)
+    g_w1[...] = acc * kappa
+    for copy in started:
+        copy.wait_send()
+    for copy in outs:
+        copy.wait()
+
+
+def fast(latent, w_in, b_in, w_out, b_out, targets, var_weight, plan):
+    members = lax.axis_size("member")
+    grid = lax.axis_size("grid")
+    planes = grid // 2
+    points, width = latent.shape[1], latent.shape[2]
+    rows = w_in.shape[0]
+    vars_ = w_out.shape[0]
+    sub = points // members
+    cw = width // members
+    share = 16 * pl.cdiv(vars_, 32 * members)
+    n_sems = (planes - 1) * 4 + (members - 1) * 8 + 2 * members + 3
+    vmem = pl.BlockSpec(memory_space=pltpu.VMEM)
+    hbm = pl.BlockSpec(memory_space=pl.ANY)
+    V = pltpu.VMEM
+    scratch = [
+        V((members, points, cw), BF), V((members, cw, points), BF), V((members, planes, 2, rows, width), BF),
+        V((points, width), F32), V((points, width), BF), V((points, width), BF), V((members, points, cw), BF),
+        V((members - 1, vars_, sub), F32), V((members, vars_, sub), F32),
+        V((members - 1, vars_, sub), BF), V((members, vars_, sub), BF), V((vars_, sub), F32),
+        V((8, LANES), F32), V((LANES, LANES), F32),
+        V((2 * members * share, width), F32), V((members * share, width), BF), V((members * share, width), BF),
+        V((members, share, width), F32), V((members, share, width), BF), V((members - 1, share, width), BF),
+        V((planes, share, width), BF), V((2, members, share, width), F32),
+        V((2, width), F32), V((2, width), F32), V((members, 2, width), F32), V((planes, 2, width), F32),
+        V((planes, 2, rows, width), F32), V((members, planes, rows, width), BF), V((members, planes, rows, width), BF),
+        V((members - 1, planes, rows, width), BF), V((members - 1, planes, rows, width), BF),
+        V((members, planes, rows, width), F32), V((planes, rows, width), BF), V((planes - 1, rows, width), BF),
+        pltpu.SemaphoreType.DMA((n_sems,)), pltpu.SemaphoreType.DMA((n_sems,)),
+        pltpu.SemaphoreType.DMA((members + 2,)), pltpu.SemaphoreType.DMA((members,)),
+    ]
+    S = jax.ShapeDtypeStruct
+    gh, g_w1, g_b1, g_w2, g_b2, g_loss = pl.pallas_call(
+        functools.partial(head_kernel, members, planes),
+        out_shape=[
+            S((1, points, width), BF), S((rows, width), F32), S((1, width), F32),
+            S((vars_, width), F32), S((1, vars_), F32), S((1, 1), F32),
+        ],
+        in_specs=[hbm, vmem, vmem, vmem, vmem, hbm, vmem],
+        out_specs=[hbm, vmem, vmem, vmem, vmem, vmem],
+        scratch_shapes=scratch,
+        compiler_params=pltpu.CompilerParams(
+            collective_id=0, has_side_effects=True, vmem_limit_bytes=60 * 1024 * 1024
+        ),
+    )(latent, w_in, b_in[None], w_out, b_out[None], targets, var_weight[None])
+    return g_loss[0, 0], gh, g_w1, g_b1[0], g_w2, g_b2[0]
+
+
+def local(latent, w_in, b_in, w_out, b_out, targets, var_weight, plan):
+    members = lax.axis_size("member")
+    grid = lax.axis_size("grid")
+    points, width = latent.shape[1], latent.shape[2]
+    whole_plan = plan.shape[0] == members - 1 and members >= 3
+    tiled = (
+        w_in.shape[0] % 16 == 0 and grid % 2 == 0 and grid >= 4
+        and points % (members * TILE) == 0 and width % (members * LANES) == 0
+        and width // members == grid * w_in.shape[0] and w_out.shape[0] <= LANES
+        and points * width <= 2048 * 1024
+    )
+    run = fast if whole_plan and tiled else shards
+    return run(latent, w_in, b_in, w_out, b_out, targets, var_weight, plan)
+
+
 def solution(mesh):
     placed = (
         P("member", "grid", None),
@@ -91,7 +489,7 @@
         P(),
     )
     return jax.shard_map(
-        shards,
+        local,
         mesh=mesh,
         in_specs=placed,
         out_specs=(P(), P("member", "grid", None), P(("member", "grid"), None), P(), P(), P()),

time: 315 us -> 101 us (0.32)
  waiting for transfers between devices: 202 us -> 0 us
  Pallas kernels: 0 us -> 90.8 us
  matrix products: 40.7 us -> 0 us
  blocking collectives: 40.3 us -> 0 us
  between operations: 15.7 us -> 2.5 us
  other arithmetic: 10.2 us -> 0 us
    all_gather x2 -> x0, waiting for transfers between devices: 107 us -> none  [the longest x1 62.1 us: shards(): w_full = lax.all_gather(w_in, ('member', 'grid'), axis=0, tiled=True)]
    psum x1 -> x0, waiting for transfers between devices: 95.1 us -> none  [shards(): summed = lax.psum(full_term, ('member', 'grid'))]
    pallas_call x0 -> x1, Pallas kernels: none -> 90.8 us  [fast(): pl.pallas_call(functools.partial(head_kernel, members, planes), out_shape...]
    dot_general x8 -> x0, matrix products: 40.7 us -> none  [the longest x1 12.6 us: shards(): jnp.dot(hidden_in, w_full, preferred_element_type=jnp.float32)]
    psum x1 -> x0, blocking collectives: 40.3 us -> none  [shards(): lax.psum((out_term, jnp.sum(cot, axis=1), jnp.sum(dpre, axis=0), jnp.sum(...]
    mul x4 -> x0, other arithmetic: 4.15 us -> none  [the longest x1 1.8 us: shards(): sum_w2 * kappa]
    div x1 -> x0, other arithmetic: 4.09 us -> none  [fold(): slope_sum = jnp.einsum('k,kvp->vp', weights, diff / root)]
    unnamed x29 -> x13, local copies, waits for them, and re-layouts: 4.93 us -> 7.23 us
  transfers between devices with their start and end apart: 3 -> 0, of which waited for: 3 -> 0; matrix products, arithmetic and copies ran while one was open for 3% -> 0% of each run, Pallas kernels for 0% -> 0%
where the time goes in v1:
time: 101 us
  Pallas kernels  90.8 us (90%)
  local copies, waits for them, and re-layouts  7.23 us (7%)
  between operations  2.5 us (2%)
    pallas_call x1, Pallas kernels, fast(): pl.pallas_call(functools.partial(head_kernel, members, planes), out_shape...  90.8 us
    unnamed x13, local copies, waits for them, and re-layouts  7.23 us

profile of v1, /device:TPU:0, one launch (start us, length us, event | category | flops | bytes accessed | tf_op | source)
XLA Modules:
  0.0 100.5 jit_solution(14532836993098260750)
XLA Ops:
  0.6 90.8 %shard_map.118 = (bf16[1,2048,1024]{2,1,0:T(8,128)(2,1)}, f32[32,1024]{1,0:T(8,128)}, f32[1,1024]{1,0:T(1,128)}, f32[100,1024]{1,0:T(8,128)}, f32[1,100]{1,0:T(1,128)}, /*index=5*/f32[1,1]{1,0:T(1,128)}) custom-call(bf16[1,2048,1024]{2,1,0:T(8,128)(2,1)} %lat_hbm.1, bf16[32,1024]{1,0:T(8,128)(2,1)} %w_in.1, f32[1,1024]{1,0:T(1,128)} %bitcast.6, ...), custom_call_target="tpu_custom_call" | custom-call | tf_op jit(solution)/shard_map/pallas_call | solution.py:449
  92.1 0.0 copy-start.1
  92.1 0.0 copy-start.2
  92.1 0.0 copy-start
  92.1 0.0 copy-start.3
  92.2 4.7 %copy.20 = bf16[1,2048,1024]{2,1,0:T(8,128)(2,1)} copy(bf16[1,2048,1024]{2,1,0:T(8,128)(2,1)} %get-tuple-element.25) | data formatting | bytes 8388608
  96.9 0.0 copy-done.1
  96.9 0.7 copy.21
  97.5 0.0 copy-done.2
  97.5 0.6 copy.22
  98.1 0.0 copy-done
  98.1 0.8 copy.23
  98.9 0.0 copy-done.3
  98.9 0.5 copy.24
Async XLA Ops:
  92.1 4.7 %copy-start.1 = (f32[32,1024]{1,0:T(8,128)S(1)}, f32[32,1024]{1,0:T(8,128)}, u32[]{:S(2)}) copy-start(f32[32,1024]{1,0:T(8,128)} %get-tuple-element.26) | copy-start | bytes 393220
  92.1 5.4 %copy-start.2 = (f32[1,1024]{1,0:T(1,128)S(1)}, f32[1,1024]{1,0:T(1,128)}, u32[]{:S(2)}) copy-start(f32[1,1024]{1,0:T(1,128)} %get-tuple-element.15) | copy-start | bytes 12292
  92.1 6.0 %copy-start = (f32[100,1024]{1,0:T(8,128)S(1)}, f32[100,1024]{1,0:T(8,128)}, u32[]{:S(2)}) copy-start(f32[100,1024]{1,0:T(8,128)} %get-tuple-element.28) | copy-start | bytes 1228804
  92.1 6.7 %copy-start.3 = (f32[1,100]{1,0:T(1,128)S(1)}, f32[1,100]{1,0:T(1,128)}, u32[]{:S(2)}) copy-start(f32[1,100]{1,0:T(1,128)} %get-tuple-element.17) | copy-start | bytes 1204

commit v2 on v1

--- a/solution.py
+++ b/solution.py
@@ -119,8 +119,11 @@
     latent = w_out.shape[1]
     total = points * planes * 2
 
+    across, down = m + 1 - 2 * lax.rem(m, 2), m + 2 - 4 * (m // 2)
+    order = (m, members - 1 - m, across, down)
+
     def mem(k):
-        return lax.rem(m + k + members, members)
+        return order[k % members]
 
     def zed(k):
         return lax.rem(z + k + planes, planes)
@@ -165,16 +168,8 @@
         pl.semaphore_signal(barrier, inc=1, device_id=dev, device_id_type=pl.DeviceIdType.MESH)
     pl.semaphore_wait(barrier, len(peers))
 
-    z_copies = [send(w_in, w_buf.at[m, z, c], z_dev(k)) for k in range(1, planes)]
-
-    for copy in loads:
-        copy.wait()
+    z_copies = [None] + [send(w_in, w_buf.at[m, z, c], z_dev(k)) for k in range(1, planes)]
     own.wait()
-    for copy in z_copies:
-        copy.wait_recv()
-    half = w_buf.at[m, :, c]
-    mem_copies = [None] + [send(half, half, member_dev(k)) for k in range(1, members)]
-    part_copies = [send(half, half, partner)]
 
     def transpose_chunk(ch):
         def body(t, carry):
@@ -183,8 +178,6 @@
             return carry
         lax.fori_loop(0, points // TILE, body, 0)
 
-    for ch in range(members):
-        transpose_chunk(ch)
     rowbuf[...] = jnp.zeros_like(rowbuf)
     rowbuf[0:1, :vars_] = b_out[...]
     rowbuf[1:2, :vars_] = vw[...]
@@ -194,17 +187,35 @@
     ot[...] = jnp.zeros_like(ot)
     sm[...] = jnp.zeros_like(sm)
 
-    for k in range(members):
-        ch = mem(-k)
-        if k > 0:
-            mem_copies[k].wait_recv()
-            got = w_buf.at[ch, :, c]
-            part_copies.append(send(got, got, partner))
-        part_copies[k].wait_recv()
-        if k == members - 1:
-            break
-
-        def body(t, carry, ch=ch, first=k == 0):
+    near = {2: [], 3: []}
+    far = []
+    to_part = {k: [] for k in range(members)}
+
+    def hand_over(k, step):
+        block = w_buf.at[mem(k), zed(-step), c]
+        to_part[k].append(send(block, block, partner))
+        return block
+
+    def spread_block(step):
+        if step > 0:
+            z_copies[step].wait_recv()
+        block = hand_over(0, step)
+        for k in (2, 3):
+            near[k].append(send(block, block, member_dev(k)))
+
+    def relay_block(step):
+        for k in (2, 3):
+            near[k][step].wait_recv()
+            block = hand_over(k, step)
+            if step % 2 == k - 2:
+                far.append(send(block, block, member_dev(5 - k)))
+
+    def contract(k, first):
+        ch = mem(k)
+        for copy in to_part[k]:
+            copy.wait_recv()
+
+        def body(t, carry):
             r0 = pl.multiple_of(t * TILE, TILE)
             w = w_buf[ch].reshape(width, latent)
             before = b_in[...] if first else gp[pl.ds(r0, TILE), :]
@@ -213,7 +224,27 @@
 
         lax.fori_loop(0, points // TILE, body, 0)
 
-    last = mem(1 - members)
+    for step in range(planes):
+        spread_block(step)
+        if step > 0:
+            relay_block(step - 1)
+        if step < members:
+            loads[step].wait()
+            transpose_chunk(step)
+    for ch in range(planes, members):
+        loads[ch].wait()
+        transpose_chunk(ch)
+    contract(0, True)
+    relay_block(planes - 1)
+    contract(2, False)
+    contract(3, False)
+    for step in range(planes):
+        far[step].wait_recv()
+        hand_over(1, step)
+    for copy in to_part[1]:
+        copy.wait_recv()
+
+    last = mem(1)
     c0 = math.sqrt(2.0 / math.pi)
     f_copies = [None]
     for k in range(1, members + 1):
@@ -222,12 +253,12 @@
         def body(t, carry, base=base):
             r0 = pl.multiple_of(base + t * TILE, TILE)
             x = dot(lat[last, pl.ds(r0, TILE), :], w_buf[last].reshape(width, latent), NN)
-            x = x + (b_in[...] if members == 1 else gp[pl.ds(r0, TILE), :])
+            x = x + gp[pl.ds(r0, TILE), :]
             sq = x * x
-            th = jnp.tanh(c0 * x * (1.0 + 0.044715 * sq))
-            cdf = 0.5 + 0.5 * th
-            act[pl.ds(r0, TILE), :] = (x * cdf).astype(BF)
-            gp[pl.ds(r0, TILE), :] = cdf + 0.5 * x * (1.0 - th * th) * (c0 + (3.0 * 0.044715 * c0) * sq)
+            cdf = 0.5 + 0.5 * jnp.tanh(x * (c0 + (0.044715 * c0) * sq))
+            out = x * cdf
+            act[pl.ds(r0, TILE), :] = out.astype(BF)
+            gp[pl.ds(r0, TILE), :] = cdf + (out * (1.0 - cdf)) * (2.0 * c0 + (6.0 * 0.044715 * c0) * sq)
             return carry
 
         lax.fori_loop(0, sub // TILE, body, 0)
@@ -275,7 +306,7 @@
             else:
                 csend[a - 1, :, cols] = cot.astype(BF)
         l_sum += scale * (miss_sum - spread * (1.0 / (members - 1)))
-    c_copies = [None] + [send(csend.at[a - 1], crecv.at[a], member_dev(-a)) for a in range(1, members)]
+    c_copies = [None] + [send(csend.at[a - 1], crecv.at[a], member_dev(a)) for a in range(1, members)]
     lane_sums[:vars_, :] = b_sum
     sm[1:2, :LANES] = jnp.sum(lane_sums[...].T, axis=0, keepdims=True)
     sm[1:2, LANES:2 * LANES] = jnp.sum(l_sum, axis=0, keepdims=True)
@@ -319,17 +350,36 @@
     def to_member(k):
         p_copies[k].wait_recv()
         m_send[k - 1] = (z_keep[k - 1] + p_recv[k - 1].astype(F32)).astype(BF)
-        return send(m_send.at[k - 1], m_recv.at[k - 1], member_dev(k))
+        m_copies[k] = [
+            send(m_send.at[k - 1, zed(step)], m_recv.at[k - 1, zed(step)], member_dev(k))
+            for step in list(range(1, planes)) + [0]
+        ]
 
     p_copies = {}
     m_copies = {}
 
     def do_chunk(k):
-        mine, copy = chunk(k)
-        z_keep[k - 1] = mine
-        p_copies[k] = copy
+        z_keep[k - 1], p_copies[k] = chunk(k)
+
+    outs = []
+
+    def hidden_grad(ch):
+        def body(t, carry):
+            r0 = pl.multiple_of(t * TILE, TILE)
+            w = w_buf[ch].reshape(width, latent)
+            gh[ch, pl.ds(r0, TILE), :] = dot(dpre[pl.ds(r0, TILE), :], w, NT).astype(BF)
+            return carry
+
+        lax.fori_loop(0, points // TILE, body, 0)
+        copy = pltpu.make_async_copy(gh.at[ch], gh_hbm.at[0, :, pl.ds(ch * width, width)], out_sem.at[ch])
+        copy.start()
+        outs.append(copy)
 
     do_chunk(1)
+    do_chunk(2)
+    to_member(1)
+    do_chunk(3)
+    to_member(2)
     op_copy.wait_recv()
     mine = pl.multiple_of(c * (members * share), share)
     om_keep[...] = (ot[pl.ds(mine, members * share), :] + op_recv[...].astype(F32)).reshape(members, share, latent)
@@ -338,8 +388,9 @@
     sp_copy.wait_recv()
     smm[m] = sm[...] + sp_recv[...]
     sm_copies = [send(smm.at[m], smm.at[m], member_dev(k)) for k in range(1, members)]
-    do_chunk(2)
-    m_copies[1] = to_member(1)
+    do_chunk(4)
+    to_member(3)
+    hidden_grad(0)
     acc = om_keep[m]
     for k in range(1, members):
         om_copies[k - 1].wait_recv()
@@ -353,9 +404,7 @@
         acc += smm[k]
     smz[z] = acc
     sz_copies = [send(smz.at[z], smz.at[z], z_dev(k)) for k in range(1, planes)]
-    for k in range(3, members):
-        do_chunk(k)
-        m_copies[k - 1] = to_member(k - 1)
+    hidden_grad(1)
     for copy in oz_copies:
         copy.wait_recv()
     acc = oz[0].astype(F32)
@@ -363,35 +412,33 @@
         acc += oz[k].astype(F32)
     w2[c, m] = acc
     w2_copies = [send(w2.at[c, m], w2.at[c, m], member_dev(k)) for k in range(1, members)]
-    do_chunk(members)
-    m_copies[members - 1] = to_member(members - 1)
+    hidden_grad(2)
+    p_copies[members].wait_recv()
+
+    def plane_sum(step):
+        at = zed(step)
+        acc = z_keep[members - 1, at] + p_recv[members - 1, at].astype(F32)
+        for k in range(1, members):
+            m_copies[k][(step - 1) % planes].wait_recv()
+            acc += m_recv[k - 1, at].astype(F32)
+        return acc
+
+    zz_copies = []
+
+    def to_plane(step):
+        z_send[step] = plane_sum(step).astype(BF)
+        zz_copies.append(send(z_send.at[step], z_recv.at[step - 1], z_dev(step)))
+
+    to_plane(1)
+    hidden_grad(3)
+    for step in range(2, planes):
+        to_plane(step)
     for copy in w2_copies:
         copy.wait_recv()
     half_copy = send(w2.at[c], w2.at[c], partner)
-
-    outs = []
-    for ch in range(members):
-        def body(t, carry, ch=ch):
-            r0 = pl.multiple_of(t * TILE, TILE)
-            w = w_buf[ch].reshape(width, latent)
-            gh[ch, pl.ds(r0, TILE), :] = dot(dpre[pl.ds(r0, TILE), :], w, NT).astype(BF)
-            return carry
-
-        lax.fori_loop(0, points // TILE, body, 0)
-        copy = pltpu.make_async_copy(gh.at[ch], gh_hbm.at[0, :, pl.ds(ch * width, width)], out_sem.at[ch])
-        copy.start()
-        outs.append(copy)
+    z_keep[members - 1, z] = plane_sum(0)
 
     kappa = 4.0 / math.sqrt(members * total)
-    p_copies[members].wait_recv()
-    acc = z_keep[members - 1] + p_recv[members - 1].astype(F32)
-    for k in range(1, members):
-        m_copies[k].wait_recv()
-        acc += m_recv[k - 1].astype(F32)
-    z_keep[members - 1] = acc
-    z_send[...] = acc.astype(BF)
-    zz_copies = [send(z_send.at[zed(k)], z_recv.at[k - 1], z_dev(k)) for k in range(1, planes)]
-
     for copy in sz_copies:
         copy.wait_recv()
     acc = smz[0]
@@ -425,7 +472,7 @@
     sub = points // members
     cw = width // members
     share = 16 * pl.cdiv(vars_, 32 * members)
-    n_sems = (planes - 1) * 4 + (members - 1) * 8 + 2 * members + 3
+    n_sems = (planes - 1) * 4 + planes * 10 + (members - 1) * 5 + members + 3
     vmem = pl.BlockSpec(memory_space=pltpu.VMEM)
     hbm = pl.BlockSpec(memory_space=pl.ANY)
     V = pltpu.VMEM
@@ -466,9 +513,9 @@
     members = lax.axis_size("member")
     grid = lax.axis_size("grid")
     points, width = latent.shape[1], latent.shape[2]
-    whole_plan = plan.shape[0] == members - 1 and members >= 3
+    whole_plan = plan.shape[0] == members - 1
     tiled = (
-        w_in.shape[0] % 16 == 0 and grid % 2 == 0 and grid >= 4
+        w_in.shape[0] % 16 == 0 and grid % 2 == 0 and grid >= 4 and members == 4
         and points % (members * TILE) == 0 and width % (members * LANES) == 0
         and width // members == grid * w_in.shape[0] and w_out.shape[0] <= LANES
         and points * width <= 2048 * 1024

time: 101 us -> 93 us (0.921)
  Pallas kernels: 90.8 us -> 83.1 us
    pallas_call x1, Pallas kernels: 90.8 us -> 83.1 us  [fast(): pl.pallas_call(functools.partial(head_kernel, members, planes), out_shape...]
where the time goes in v2:
time: 93 us; the launch traced here: 92.8 us
  Pallas kernels  83.1 us (89%)
  local copies, waits for them, and re-layouts  7.23 us (8%)
  between operations  2.5 us (3%)
    pallas_call x1, Pallas kernels, fast(): pl.pallas_call(functools.partial(head_kernel, members, planes), out_shape...  83.1 us
    unnamed x13, local copies, waits for them, and re-layouts  7.23 us

profile of v2, /device:TPU:0, one launch (start us, length us, event | category | flops | bytes accessed | tf_op | source)
XLA Modules:
  0.0 92.8 jit_solution(7233609556595909505)
XLA Ops:
  0.6 83.1 %shard_map.118 = (bf16[1,2048,1024]{2,1,0:T(8,128)(2,1)}, f32[32,1024]{1,0:T(8,128)}, f32[1,1024]{1,0:T(1,128)}, f32[100,1024]{1,0:T(8,128)}, f32[1,100]{1,0:T(1,128)}, /*index=5*/f32[1,1]{1,0:T(1,128)}) custom-call(bf16[1,2048,1024]{2,1,0:T(8,128)(2,1)} %lat_hbm.1, bf16[32,1024]{1,0:T(8,128)(2,1)} %w_in.1, f32[1,1024]{1,0:T(1,128)} %bitcast.6, ...), custom_call_target="tpu_custom_call" | custom-call | tf_op jit(solution)/shard_map/pallas_call | solution.py:496
  84.4 0.0 copy-start.1
  84.4 0.0 copy-start.2
  84.4 0.0 copy-start
  84.5 0.0 copy-start.3
  84.5 4.7 %copy.20 = bf16[1,2048,1024]{2,1,0:T(8,128)(2,1)} copy(bf16[1,2048,1024]{2,1,0:T(8,128)(2,1)} %get-tuple-element.25) | data formatting | bytes 8388608
  89.2 0.0 copy-done.1
  89.2 0.7 copy.21
  89.8 0.0 copy-done.2
  89.8 0.6 copy.22
  90.4 0.0 copy-done
  90.4 0.8 copy.23
  91.2 0.0 copy-done.3
  91.2 0.5 copy.24
Async XLA Ops:
  84.4 4.7 %copy-start.1 = (f32[32,1024]{1,0:T(8,128)S(1)}, f32[32,1024]{1,0:T(8,128)}, u32[]{:S(2)}) copy-start(f32[32,1024]{1,0:T(8,128)} %get-tuple-element.26) | copy-start | bytes 393220
  84.4 5.4 %copy-start.2 = (f32[1,1024]{1,0:T(1,128)S(1)}, f32[1,1024]{1,0:T(1,128)}, u32[]{:S(2)}) copy-start(f32[1,1024]{1,0:T(1,128)} %get-tuple-element.15) | copy-start | bytes 12292
  84.4 6.0 %copy-start = (f32[100,1024]{1,0:T(8,128)S(1)}, f32[100,1024]{1,0:T(8,128)}, u32[]{:S(2)}) copy-start(f32[100,1024]{1,0:T(8,128)} %get-tuple-element.28) | copy-start | bytes 1228804
  84.5 6.7 %copy-start.3 = (f32[1,100]{1,0:T(1,128)S(1)}, f32[1,100]{1,0:T(1,128)}, u32[]{:S(2)}) copy-start(f32[1,100]{1,0:T(1,128)} %get-tuple-element.17) | copy-start | bytes 1204
